TPU v7x, 128 devices: a whole 4x4x4 slice. The times are simulated.
128 devices in a mesh: ctx: 32 (over y, z, core), head: 4 (over x).
Axes of the slice: x: 4, y: 4, z: 4, core: 2. Of those that a mesh axis runs over, the one named last changes fastest.
Arguments:
- stream: bfloat16 [16384, 2048], P(('ctx', 'head')), may hold values from -6 to 6
- moe_gain: float32 [2048], replicated, may hold values from 0.5 to 1.5
- router: bfloat16 [2048, 256], replicated, may hold values from -0.125 to 0.125
- expert_ids: int32 [16384, 10], P(('ctx', 'head')), may hold values from 0 to 255, all different within a row; in each aligned block of 128 rows (0 to 127, 128 to 255, ...) at most 6 rows name the same one
- expert_gate: bfloat16 [256, 2048, 512], P(('ctx', 'head')), may hold values from -0.125 to 0.125
- expert_up: bfloat16 [256, 2048, 512], P(('ctx', 'head')), may hold values from -0.125 to 0.125
- expert_down: bfloat16 [256, 512, 2048], P(('ctx', 'head')), may hold values from -1 to 1
- mixer_gain: float32 [2048], replicated, may hold values from 0.5 to 1.5
- query_weight: bfloat16 [2048, 1024], P(None, 'head'), may hold values from -0.125 to 0.125
- key_weight: bfloat16 [2048, 1024], P(None, 'head'), may hold values from -0.125 to 0.125
- value_weight: bfloat16 [2048, 2048], P(None, 'head'), may hold values from -0.125 to 0.125
- output_gate: bfloat16 [2048, 2048], P(None, 'head'), may hold values from -0.125 to 0.125
- beta_weight: bfloat16 [2048, 16], P(None, 'head'), may hold values from -0.125 to 0.125
- decay_weight: bfloat16 [2048, 16], P(None, 'head'), may hold values from -0.5 to 0.5
- query_conv: float32 [4, 1024], P(None, 'head'), may hold values from -3 to 3
- key_conv: float32 [4, 1024], P(None, 'head'), may hold values from -3 to 3
- value_conv: float32 [4, 2048], P(None, 'head'), may hold values from -3 to 3
- decay_log: float32 [16], P('head'), may hold values from -12 to -2.5
- decay_bias: float32 [16], P('head'), may hold values from -2 to 1
- head_gain: float32 [128], replicated, may hold values from 0.5 to 1.5
- out_weight: bfloat16 [2048, 2048], P('head'), may hold values from -0.125 to 0.125
Outputs:
- moe_out: bfloat16 [16384, 2048], P(('ctx', 'head'))
- mixer_out: bfloat16 [16384, 2048], P(('ctx', 'head'))
Inputs may be any that keep to these rules, and one draw needn't show every extreme that they name: `expert_ids`: each row names 10 different experts; in each aligned block of 128 rows (the rows of one device) no expert is named by more than 6 rows, a bound that some block reaches.
All inputs are finite; a program needn't handle non-finite values.
Results may differ from a plain program's by a relative error of at most 0.017.
Values may be sent and summed in bfloat16 or wider, within the bound.
A program may use at most 128 MiB of HBM per device.

v0:
```python
import math
import jax
import jax.numpy as jnp
from jax import lax
from jax.sharding import PartitionSpec as P

DK = 128
epsilon = 1e-06
exact_precision = lax.Precision.HIGHEST


def passed_along(value, axis, steps):
    count = lax.axis_size(axis)
    first, last = (max(0, -steps), min(count, count - steps))
    return lax.ppermute(value, axis, [(source, source + steps) for source in range(first, last)])


def prefix(array, axis, combine, identity):
    peers, place = (lax.axis_size(axis), lax.axis_index(axis))
    everything = jax.tree.map(
        lambda part, kind: lax.all_gather(part.astype(kind), axis),
        array,
        (jnp.bfloat16, jnp.bfloat16),
    )
    start = jax.tree.map(
        lambda part, zero: jnp.broadcast_to(jnp.asarray(zero, part.dtype), part.shape),
        array,
        identity,
    )

    def step(k, before):
        reached = k < place
        new = combine(
            before, jax.tree.map(lambda part, own: part[k].astype(own.dtype), everything, array)
        )
        return jax.tree.map(lambda a, b: jnp.where(reached, a, b), new, before)

    return lax.fori_loop(0, peers, step, start)


def rms_rows(values, gain):
    values = values.astype(jnp.float32)
    scale = lax.rsqrt(jnp.mean(values * values, axis=-1, keepdims=True) + epsilon)
    return values * scale * gain


def block_terms(queries, key_rows, values, strength, decays):
    length = queries.shape[0]
    cumulative = jnp.cumsum(decays)
    spread = cumulative[:, None] - cumulative[None, :]
    positions = jnp.arange(length, dtype=jnp.int32)
    strict = positions[:, None] > positions[None, :]
    inclusive = positions[:, None] >= positions[None, :]
    fall_strict = jnp.where(strict, jnp.exp(jnp.where(strict, spread, 0.0)), 0.0)
    fall_inclusive = jnp.where(inclusive, jnp.exp(jnp.where(inclusive, spread, 0.0)), 0.0)
    key_dots = jnp.dot(key_rows, key_rows.T, precision=exact_precision)
    strict_part = strength[:, None] * fall_strict * key_dots
    system = jnp.eye(length, dtype=jnp.float32) + strict_part
    targets = strength[:, None] * jnp.concatenate(
        [values, jnp.exp(cumulative)[:, None] * key_rows], axis=1
    )
    solved = jax.scipy.linalg.solve_triangular(system, targets, lower=True, unit_diagonal=True)
    value_width = values.shape[1]
    w_values = solved[:, :value_width]
    w_keys = solved[:, value_width:]
    mixing = fall_inclusive * jnp.dot(queries, key_rows.T, precision=exact_precision)
    q_decayed = jnp.exp(cumulative)[:, None] * queries
    k_decayed = jnp.exp(cumulative[-1] - cumulative)[:, None] * key_rows
    closing = jnp.exp(cumulative[-1])
    return (w_values, w_keys, mixing, q_decayed, k_decayed, closing)


def local_pass(queries, key_rows, values, strength, decays):
    length = queries.shape[0]
    block_len = math.gcd(length, 64)
    block_count = length // block_len

    def split_blocks(array):
        return array.reshape((block_count, block_len) + array.shape[1:])

    terms = jax.vmap(block_terms)(
        split_blocks(queries),
        split_blocks(key_rows),
        split_blocks(values),
        split_blocks(strength),
        split_blocks(decays),
    )

    def advance(carried_pair, block_term):
        state_now, transfer = carried_pair
        w_values, w_keys, mixing, q_decayed, k_decayed, closing = block_term
        update = w_values - jnp.dot(w_keys, state_now, precision=exact_precision)
        result = jnp.dot(q_decayed, state_now, precision=exact_precision) + jnp.dot(
            mixing, update, precision=exact_precision
        )
        moved_rows = jnp.dot(w_keys, transfer, precision=exact_precision)
        reading = jnp.dot(q_decayed, transfer, precision=exact_precision) - jnp.dot(
            mixing, moved_rows, precision=exact_precision
        )
        state_now = closing * state_now + jnp.dot(k_decayed.T, update, precision=exact_precision)
        transfer = closing * transfer - jnp.dot(k_decayed.T, moved_rows, precision=exact_precision)
        return ((state_now, transfer), (result, reading))

    key_width = key_rows.shape[1]
    initial = (
        jnp.zeros((key_width, values.shape[1]), jnp.float32),
        jnp.eye(key_width, dtype=jnp.float32),
    )
    (state_now, transfer), (results, read_values) = lax.scan(advance, initial, terms)
    return (results.reshape(length, -1), read_values.reshape(length, -1), transfer, state_now)


def unit_heads(array, heads):
    reshaped_rows = array.reshape(array.shape[0], heads, -1)
    return reshaped_rows * lax.rsqrt(
        jnp.sum(reshaped_rows * reshaped_rows, axis=-1, keepdims=True) + epsilon
    )


def on_device(
    stream,
    moe_gain,
    router,
    expert_ids,
    expert_gate,
    expert_up,
    expert_down,
    mixer_gain,
    query_weight,
    key_weight,
    value_weight,
    output_gate,
    beta_weight,
    decay_weight,
    query_conv,
    key_conv,
    value_conv,
    decay_log,
    decay_bias,
    head_gain,
    out_weight,
):
    ctx_count = lax.axis_size("ctx")
    head_count = lax.axis_size("head")
    sources = ctx_count * head_count
    tok_rows, model_width = stream.shape
    top_count = expert_ids.shape[1]
    local_experts = expert_gate.shape[0]
    experts_all = local_experts * sources
    capacity = (11 * tok_rows * top_count + 10 * experts_all - 1) // (10 * experts_all)
    normed = rms_rows(stream, moe_gain).astype(jnp.bfloat16)
    logits = jnp.dot(normed, router, preferred_element_type=jnp.float32)
    chosen = jnp.take_along_axis(logits, expert_ids, axis=1)
    raised = jnp.exp(chosen)
    weights = raised / jnp.sum(raised, axis=1, keepdims=True)
    flat_ids = expert_ids.reshape(-1)
    matches = (flat_ids[:, None] == jnp.arange(experts_all, dtype=jnp.int32)[None, :]).astype(
        jnp.int32
    )
    slot_index = jnp.sum((jnp.cumsum(matches, axis=0) - 1) * matches, axis=1)
    places = flat_ids * capacity + slot_index
    token_rows = jnp.arange(tok_rows * top_count, dtype=jnp.int32) // top_count
    outgoing = (
        jnp.zeros((experts_all * capacity, model_width), jnp.bfloat16)
        .at[places]
        .set(normed[token_rows])
    )
    outgoing = outgoing.reshape(sources, local_experts, capacity, model_width)
    received = lax.all_to_all(outgoing, ("ctx", "head"), split_axis=0, concat_axis=0, tiled=True)
    gate_part = jnp.einsum(
        "nesd,edh->nesh", received, expert_gate, preferred_element_type=jnp.float32
    )
    up_part = jnp.einsum("nesd,edh->nesh", received, expert_up, preferred_element_type=jnp.float32)
    hidden = (jax.nn.silu(gate_part) * up_part).astype(jnp.bfloat16)
    returned = lax.all_to_all(
        jnp.einsum(
            "nesh,ehd->nesd", hidden, expert_down, preferred_element_type=jnp.float32
        ).astype(jnp.bfloat16),
        ("ctx", "head"),
        split_axis=0,
        concat_axis=0,
        tiled=True,
    )
    gathered_rows = returned.reshape(experts_all * capacity, model_width)[places].reshape(
        tok_rows, top_count, model_width
    )
    moe_out = jnp.sum(weights[:, :, None] * gathered_rows.astype(jnp.float32), axis=1).astype(
        jnp.bfloat16
    )
    mixer_in = rms_rows(
        stream.astype(jnp.float32) + moe_out.astype(jnp.float32), mixer_gain
    ).astype(jnp.bfloat16)
    weight_list = (query_weight, key_weight, value_weight, output_gate, beta_weight, decay_weight)
    piece_rows = lax.all_gather(mixer_in, "head", axis=0, tiled=True)
    projected = jnp.concatenate(
        [jnp.dot(piece_rows, matrix, preferred_element_type=jnp.float32) for matrix in weight_list],
        axis=1,
    )
    row_count = projected.shape[0]
    key_cols = query_weight.shape[1]
    value_cols = value_weight.shape[1]
    head_cols = beta_weight.shape[1]
    conv_cols = 2 * key_cols + value_cols
    qkv_raw = projected[:, :conv_cols].astype(jnp.bfloat16)
    gate_raw = projected[:, conv_cols : conv_cols + value_cols].astype(jnp.bfloat16)
    beta_raw = projected[:, conv_cols + value_cols : conv_cols + value_cols + head_cols]
    decay_raw = projected[:, conv_cols + value_cols + head_cols :]
    taps = jnp.concatenate([query_conv, key_conv, value_conv], axis=1)
    rim_len = taps.shape[0] - 1
    rim_cells = passed_along(qkv_raw[row_count - rim_len :], "ctx", 1)
    extended = jnp.concatenate([rim_cells.astype(jnp.float32), qkv_raw.astype(jnp.float32)], axis=0)
    summed = jnp.zeros((row_count, conv_cols), jnp.float32)
    for shift_index in range(rim_len + 1):
        summed = (
            summed + taps[shift_index][None, :] * extended[shift_index : shift_index + row_count]
        )
    convolved = jax.nn.silu(summed)
    key_width = DK
    key_heads = key_cols // key_width
    group_size = head_cols // key_heads
    queries = unit_heads(convolved[:, :key_cols], key_heads) * key_width ** (-0.5)
    key_rows = unit_heads(convolved[:, key_cols : 2 * key_cols], key_heads)
    values = convolved[:, 2 * key_cols :].reshape(row_count, head_cols, -1)
    strength = jax.nn.sigmoid(beta_raw)
    decays = -jnp.exp(decay_log)[None, :] * jax.nn.softplus(decay_raw + decay_bias[None, :])
    query_heads = jnp.repeat(queries, group_size, axis=1).transpose(1, 0, 2)
    key_head_rows = jnp.repeat(key_rows, group_size, axis=1).transpose(1, 0, 2)
    output_list, read_values, transfer, offset = jax.vmap(local_pass)(
        query_heads, key_head_rows, values.transpose(1, 0, 2), strength.T, decays.T
    )

    def compose(earlier, later):
        joined = jnp.einsum("hij,hjk->hik", later[0], earlier[0], precision=exact_precision)
        shifted = (
            jnp.einsum("hij,hjk->hik", later[0], earlier[1], precision=exact_precision) + later[1]
        )
        return (joined, shifted)

    identity = (
        jnp.broadcast_to(jnp.eye(transfer.shape[1], dtype=jnp.float32), transfer.shape),
        jnp.zeros_like(offset),
    )
    incoming_rows = prefix((transfer, offset), "ctx", compose, identity)[1]
    delta_core_output = output_list + jnp.einsum(
        "wnc,wcg->wng", read_values, incoming_rows, precision=exact_precision
    )
    delta_core_output = delta_core_output.transpose(1, 0, 2)
    normal = (
        delta_core_output
        * lax.rsqrt(
            jnp.mean(delta_core_output * delta_core_output, axis=-1, keepdims=True) + epsilon
        )
        * head_gain
    )
    gate_values = gate_raw.astype(jnp.float32).reshape(row_count, head_cols, -1)
    gated_out = (
        (normal * jax.nn.silu(gate_values)).astype(jnp.bfloat16).reshape(row_count, value_cols)
    )
    mixer_out = lax.psum_scatter(
        jnp.dot(gated_out, out_weight, preferred_element_type=jnp.float32).astype(jnp.bfloat16),
        "head",
        scatter_dimension=0,
        tiled=True,
    )
    return (moe_out, mixer_out)


def solution(mesh):
    return jax.shard_map(
        on_device,
        mesh=mesh,
        in_specs=(
            P(("ctx", "head"), None),
            P(),
            P(),
            P(("ctx", "head"), None),
            P(("ctx", "head"), None, None),
            P(("ctx", "head"), None, None),
            P(("ctx", "head"), None, None),
            P(),
            P(None, "head"),
            P(None, "head"),
            P(None, "head"),
            P(None, "head"),
            P(None, "head"),
            P(None, "head"),
            P(None, "head"),
            P(None, "head"),
            P(None, "head"),
            P("head"),
            P("head"),
            P(),
            P("head", None),
        ),
        out_specs=(P(("ctx", "head"), None), P(("ctx", "head"), None)),
        check_vma=False,
    )
```

profile of v0, /device:TPU:1, one launch (start us, length us, event | category | flops | bytes accessed | tf_op | source)
XLA Modules:
  0.0 852.3 jit_solution(13656351736903203024)
XLA Ops:
  11.0 1.8 add_add_fusion
  12.8 1.8 copy.130
  15.2 1.7 fusion.90
  17.1 34.2 %scatter_custom_fusion = bf16[1536,2048]{1,0:T(8,128)(2,1)} fusion(s32[1280]{0:T(1024)S(1)} %fusion.111, bf16[128,2048]{1,0:T(8,128)(2,1)S(1)} %fusion.102, s32[2048]{0:T(1024)S(1)} %pad_clamp_fusion.1, bf16[]{:T(256)} %constant.111.clone.1), kind=kCustom, calls=%fused_computation.65 | custom fusion | bytes 6291458 | tf_op jit(solution)/shard_map/scatter | solution.py:166
  51.3 11.0 %reshape.241 = bf16[128,2,6,2048]{3,2,1,0:T(8,128)(2,1)} reshape(bf16[1536,2048]{1,0:T(8,128)(2,1)} %scatter_custom_fusion) | data formatting | bytes 12582912 | tf_op jit(solution)/shard_map/reshape | solution.py:168
  62.3 9.6 %copy.131 = bf16[128,2,6,2048]{3,1,2,0:T(2,128)(2,1)S(1)} copy(bf16[128,2,6,2048]{3,2,1,0:T(8,128)(2,1)} %reshape.241) | data formatting | bytes 12582912 | tf_op jit(solution)/shard_map/reshape | solution.py:168
  72.0 87.2 %all_to_all.10 = bf16[128,2,6,2048]{3,1,2,0:T(2,128)(2,1)S(1)} all-to-all(bf16[128,2,6,2048]{3,1,2,0:T(2,128)(2,1)S(1)} %copy.131), channel_id=1, replica_groups=mesh['ctx'=32,'head'=4] {'ctx','head'}, dimensions={0} | all-to-all | bytes 12582912 | tf_op jit(solution)/shard_map/all_to_all | solution.py:169
  159.2 2.6 copy-done.7
  161.9 8.6 %fusion.48 = f32[2,128,6,512]{3,1,2,0:T(8,128)} fusion(bf16[128,2,6,2048]{3,1,2,0:T(2,128)(2,1)S(1)} %all_to_all.10, bf16[2,2048,512]{2,1,0:T(8,128)(2,1)S(1)} %copy-done.22), kind=kOutput, calls=%fused_computation.61 | convolution fusion | flops 3221225472 | bytes 13631488 | tf_op jit(solution)/shard_map/nesd,edh->nesh/dot_general | solution.py:173
  170.4 19.9 %convert_bitcast_fusion = bf16[128,2,6,2048]{3,0,2,1:T(8,128)(2,1)} fusion(bf16[2,512,2048]{2,1,0:T(8,128)(2,1)} %param.31, f32[2,128,6,512]{3,1,2,0:T(8,128)} %fusion.48, bf16[2,2048,512]{2,1,0:T(8,128)(2,1)} %param.29, bf16[128,2,6,2048]{3,1,2,0:T(2,128)(2,1)} %copy-done.7), kind=kOutput, calls=%fused_computation.60 | convolution fusion | flops 6450315264 | bytes 24117248 | tf_op jit(solution)/shard_map/nesh,ehd->nesd/dot_general | solution.py:176
  190.3 12.8 %copy.134 = bf16[128,2,6,2048]{3,1,2,0:T(2,128)(2,1)} copy(bf16[128,2,6,2048]{3,0,2,1:T(8,128)(2,1)} %convert_bitcast_fusion) | data formatting | bytes 12582912 | tf_op jit(solution)/shard_map/convert_element_type | solution.py:178
  203.1 4.9 all-to-all-start.1
  208.3 1.5 fusion.119
  209.9 10.3 %gather_fusion.1 = f32[1280]{0:T(1024)S(1)} fusion(f32[128,256]{1,0:T(8,128)S(1)} %fusion.119, s32[1280]{0:T(1024)S(1)} %reshape.277), kind=kCustom, calls=%fused_computation.2 | custom fusion | bytes 20480 | tf_op jit(solution)/shard_map/jit(take_along_axis)/gather | solution.py:153
  220.6 64.5 %all-to-all-done.1 = bf16[128,2,6,2048]{3,1,2,0:T(2,128)(2,1)} async-done(((bf16[128,2,6,2048]{3,1,2,0:T(2,128)(2,1)}), bf16[128,2,6,2048]{3,1,2,0:T(2,128)(2,1)}, u32[]{:S(2)}, u32[]{:S(2)}) %all-to-all-start.1) | async-done | bytes 6291488 | tf_op jit(solution)/shard_map/all_to_all | solution.py:175
  285.0 10.4 %copy.135 = bf16[128,2,6,2048]{3,2,1,0:T(8,128)(2,1)} copy(bf16[128,2,6,2048]{3,1,2,0:T(2,128)(2,1)} %all-to-all-done.1) | data formatting | bytes 12582912 | tf_op jit(solution)/shard_map/all_to_all | solution.py:175
  295.4 11.0 %reshape.242 = bf16[1536,2048]{1,0:T(8,128)(2,1)} reshape(bf16[128,2,6,2048]{3,2,1,0:T(8,128)(2,1)} %copy.135) | data formatting | bytes 12582912 | tf_op jit(solution)/shard_map/reshape | solution.py:184
  306.5 14.4 %gather_fusion = bf16[1280,2048]{1,0:T(8,128)(2,1)} fusion(bf16[1536,2048]{1,0:T(8,128)(2,1)} %reshape.242, s32[2048]{0:T(1024)S(1)} %pad_clamp_fusion), kind=kCustom, calls=%fused_computation.1 | custom fusion | bytes 10490880 | tf_op jit(solution)/shard_map/gather | solution.py:184
  320.9 10.5 %reshape.258 = f32[128,10,2048]{2,1,0:T(8,128)} reshape(bf16[1280,2048]{1,0:T(8,128)(2,1)} %gather_fusion) | data formatting | bytes 15728640 | tf_op jit(solution)/shard_map/convert_element_type | solution.py:187
  331.4 9.6 %multiply_reduce_fusion = bf16[128,2048]{1,0:T(8,128)(2,1)S(1)} fusion(f32[128,10,2048]{2,1,0:T(8,128)} %reshape.258, f32[128,10]{1,0:T(8,128)S(1)} %copy.125), kind=kLoop, calls=%fused_computation.59 | loop fusion | flops 4980736 | bytes 11015168 | tf_op jit(solution)/shard_map/reduce_sum | solution.py:187
  343.9 27.1 %all-gather.6.cloned.1.call-done = bf16[512,2048]{1,0:T(8,128)(2,1)} async-done(((bf16[128,2048]{1,0:T(8,128)(2,1)}), bf16[512,2048]{1,0:T(8,128)(2,1)}) %all-gather.6.cloned.1.call-update) | async-done | bytes 2097168 | tf_op jit(solution)/shard_map/all_gather | solution.py:194
  370.9 3.7 convolution_convert_fusion.2
  376.7 1.7 pad_maximum_fusion.1
  378.5 3.7 collective-permute-start
  384.4 2.3 fusion.94
  387.5 6.4 divide_multiply_fusion
  399.4 3.6 fusion.88
  403.0 158.7 %custom-call.4 = f32[4,8,1,64,64]{3,4,2,1,0:T(8,128)} custom-call(f32[4,8,1,64,64]{4,3,2,1,0:T(8,128)} %fusion.88), custom_call_target="InvertDiagBlocksLowerTriangular" | custom-call | tf_op jit(solution)/shard_map/vmap(vmap(jit(_solve_triangular)))/triangular_solve | solution.py:62
  564.3 1.7 broadcast_multiply_fusion
  566.5 2.4 fusion.70
  568.9 1.6 slice_bitcast_fusion
  570.5 2.8 fusion.84
  573.3 100.6 %while.31 = (s32[]{:T(128)}, f32[4,128,128]{2,1,0:T(8,128)S(1)}, f32[4,128,128]{2,1,0:T(8,128)S(1)}, f32[8,4,64,128]{3,2,0,1:T(8,128)}, f32[8,4,64,128]{3,2,0,1:...) while((s32[]{:T(128)}, f32[4,128,128]{2,1,0:T(8,128)S(1)}, ...), condition=%wide.region_12.13_spmd.clone, body=%wide.region_11.12_spmd.clone.sunk | while | flops 352878592 | bytes 4855501 | solution.py:109
  575.8 1.9 fusion.192
  580.2 1.9 fusion.194
  584.3 1.5 convolution_subtract_fusion.6
  588.4 1.9 fusion.192
  592.8 1.9 fusion.194
  596.9 1.5 convolution_subtract_fusion.6
  601.0 1.9 fusion.192
  605.3 1.9 fusion.194
  609.5 1.5 convolution_subtract_fusion.6
  613.5 1.9 fusion.192
  617.9 1.9 fusion.194
  622.0 1.5 convolution_subtract_fusion.6
  626.1 1.9 fusion.192
  630.5 1.9 fusion.194
  634.6 1.5 convolution_subtract_fusion.6
  638.7 1.9 fusion.192
  643.0 1.9 fusion.194
  647.2 1.5 convolution_subtract_fusion.6
  651.3 1.9 fusion.192
  655.6 1.9 fusion.194
  659.8 1.5 convolution_subtract_fusion.6
  663.8 1.9 fusion.192
  668.2 1.9 fusion.194
  675.7 4.3 convolution_convert_fusion.1
  680.0 1.6 copy.149
  681.6 39.2 %all-gather.8.cloned.1.call-done = bf16[128,128,128]{2,1,0:T(8,128)(2,1)} async-done(((bf16[4,128,128]{2,1,0:T(8,128)(2,1)}), bf16[128,128,128]{2,1,0:T(8,128)(2,1)}) %all-gather.8.cloned.1.call-update) | async-done | bytes 4194320 | tf_op jit(solution)/shard_map/all_gather | solution.py:21
  720.8 48.0 %all-gather.10.cloned.1.call-done = bf16[128,128,128]{2,1,0:T(8,128)(2,1)} async-done(((bf16[4,128,128]{2,1,0:T(8,128)(2,1)}), bf16[128,128,128]{2,1,0:T(8,128)(2,1)}) %all-gather.10.cloned.1.call-update) | async-done | bytes 4194320 | tf_op jit(solution)/shard_map/all_gather | solution.py:21
  768.8 42.3 %while.32 = (s32[]{:T(128)}, f32[4,128,128]{2,1,0:T(8,128)S(1)}, s32[]{:T(128)}, bf16[32,4,128,128]{3,2,1,0:T(8,128)(2,1)}, bf16[32,4,128,128]{3,2,1,0:T(8,128)(2,1)}, /*index=5*/s32[]{:T(128)}, s32[]{:T(128)}) while((s32[]{:T(128)}, f32[4,128,128]{2,1,0:T(8,128)S(1)}, s32[]{:T(128)}, bf16[32,4,128,128]{3,2,1,0:T(8,128)(2,1)}, ...), condition=%wide.region_14.15_spmd.clone, body=%wide.region_13.14_spmd.clone.sunk | while | flops 100990976 | bytes 1575519 | solution.py:38
  811.1 2.4 multiply_reduce_fusion.1
  814.0 2.6 convolution_convert_fusion
  816.6 28.7 %reduce-scatter.2.cloned.1.call-done = bf16[128,2048]{1,0:T(8,128)(2,1)} async-done(((bf16[512,2048]{1,0:T(8,128)(2,1)}), bf16[128,2048]{1,0:T(8,128)(2,1)}) %reduce-scatter.2.cloned.1.call-update) | async-done | bytes 524304 | tf_op jit(solution)/shard_map/reduce_scatter | solution.py:259
  (242 shorter events, 123.5 us)
Async XLA Ops:
  7.2 806.8 %copy-start = (bf16[512,2048]{1,0:T(8,128)(2,1)S(1)}, bf16[512,2048]{1,0:T(8,128)(2,1)}, u32[]{:S(2)}) copy-start(bf16[512,2048]{1,0:T(8,128)(2,1)} %param.45) | copy-start | bytes 6291460
  9.6 1.3 copy-start.4
  12.8 2.1 copy-start.6
  12.8 4.1 copy-start.15
  72.0 89.9 %copy-start.22 = (bf16[2,2048,512]{2,1,0:T(8,128)(2,1)S(1)}, bf16[2,2048,512]{2,1,0:T(8,128)(2,1)}, u32[]{:S(2)}) copy-start(bf16[2,2048,512]{2,1,0:T(8,128)(2,1)} %param.30) | copy-start | bytes 12582916
  159.2 2.6 copy-start.7
  203.1 5.0 copy-start.12
  203.1 82.0 %all-to-all-start.1 = ((bf16[128,2,6,2048]{3,1,2,0:T(2,128)(2,1)}), bf16[128,2,6,2048]{3,1,2,0:T(2,128)(2,1)}, u32[]{:S(2)}, u32[]{:S(2)}) async-start(bf16[128,2,6,2048]{3,1,2,0:T(2,128)(2,1)} %copy.134), calls=%async_computation.1 | async-start | bytes 12582912 | tf_op jit(solution)/shard_map/all_to_all | solution.py:175
  208.0 162.9 %all-gather.6.cloned.1.call-start = ((), (), s32[]{:S(2)}) async-start(), calls=%async_computation.3 | async-start | bytes 2621440 | tf_op jit(solution)/shard_map/all_gather | solution.py:194
  331.4 9.9 %copy-start.16 = (f32[2048]{0:T(1024)S(1)}, f32[2048]{0:T(1024)}, u32[]{:S(2)}) copy-start(f32[2048]{0:T(1024)} %param.32) | copy-start | bytes 24580
  341.0 33.6 %copy-start.8 = (bf16[128,2048]{1,0:T(8,128)(2,1)}, bf16[128,2048]{1,0:T(8,128)(2,1)S(1)}, u32[]{:S(2)}) copy-start(bf16[128,2048]{1,0:T(8,128)(2,1)S(1)} %multiply_reduce_fusion) | copy-start | bytes 1572868
  341.0 1.5 copy-start.18
  341.0 1.5 copy-start.19
  341.0 1.5 copy-start.17
  341.0 2.1 copy-start.25
  342.4 378.5 %all-gather.8.cloned.1.call-start = ((), (), s32[]{:S(2)}) async-start(), calls=%async_computation.5 | async-start | bytes 4325376 | tf_op jit(solution)/shard_map/all_gather | solution.py:21
  370.9 3.7 copy-start.5
  370.9 3.7 copy-start.23
  374.6 1.2 copy-start.24
  376.6 5.6 copy-start.13
  376.7 5.6 copy-start.21
  378.4 6.0 copy-start.14
  378.5 8.9 %collective-permute-start = (bf16[3,1024]{0,1:T(8,128)(2,1)S(1)}, bf16[3,1024]{0,1:T(8,128)(2,1)S(1)}, u32[]{:S(2)}, u32[]{:S(2)}) collective-permute-start(bf16[3,1024]{0,1:T(8,128)(2,1)S(1)} %slice.81), channel_id=1, source_target_pairs={{0,4},{4,8},{8,12},{12,16},{16,20},{20,24},{24,28},{28,32},{32,36}... | collective-permute-start | bytes 18440 | tf_op jit(solution)/shard_map/ppermute | solution.py:15
  393.9 1.3 copy-start.1
  397.2 164.4 %slice-start = ((f32[512,1024]{0,1:T(8,128)}), f32[512,512]{0,1:T(8,128)S(1)}, s32[]{:S(2)}) async-start(f32[512,1024]{0,1:T(8,128)} %copy-done.1), calls=%async_computation.7 | async-start | bytes 2097152 | tf_op jit(solution)/shard_map/slice | solution.py:223
  398.4 1.0 copy-start.2
  562.9 1.4 copy-start.3
  564.3 1.7 copy-start.9
  564.3 2.2 copy-start.10
  674.6 94.2 %all-gather.10.cloned.1.call-start = ((), (), s32[]{:S(2)}) async-start(), calls=%async_computation.6 | async-start | bytes 4325376 | tf_op jit(solution)/shard_map/all_gather | solution.py:21
  675.3 170.0 %reduce-scatter.2.cloned.1.call-start = ((), (), s32[]{:S(2)}) async-start(), calls=%async_computation.4 | async-start | bytes 2621440 | tf_op jit(solution)/shard_map/reduce_scatter | solution.py:259
  811.1 2.4 copy-start.11
  811.1 2.4 copy-start.20
Sparse Core Ops, SparseCore 0:
  342.5 28.4 all-gather.5
  674.7 46.0 all-gather.7
  723.1 45.6 all-gather.9
  816.7 28.5 reduce-scatter.1
where the time goes:
time: 859 us; the launch traced here: 852 us
  waiting for transfers between devices  208 us (24%)
  matrix products  191 us (22%)
  other arithmetic  189 us (22%)
  local copies, waits for them, and re-layouts  152 us (18%)
  blocking collectives  87.2 us (10%)
  between operations  14.9 us (2%)
  starting transfers between devices  9.12 us (1%)
    another operation x2, other arithmetic, block_terms(): jax.scipy.linalg.solve_triangular(system, targets, lower=True, unit_diago...  159 us
    all_to_all x1, blocking collectives, on_device(): lax.all_to_all(outgoing, ('ctx', 'head'), split_axis=0, concat_axis=0, ti...  87.2 us
    all_gather x2, waiting for transfers between devices, prefix(): lax.all_gather(part.astype(kind), axis)  87.2 us
    all_to_all x1, waiting for transfers between devices, on_device(): lax.all_to_all(jnp.einsum('nesh,ehd->nesd', hidden, expert_down, preferre...  64.5 us
    dot_general x32, matrix products, compose(): jnp.einsum('hij,hjk->hik', later[0], earlier[1], precision=exact_precision)  40.5 us
    scatter x1, local copies, waits for them, and re-layouts, on_device(): outgoing = jnp.zeros((experts_all * capacity, model_width), jnp.bfloat16)...  34.2 us
    reduce_scatter x1, waiting for transfers between devices, on_device(): lax.psum_scatter(jnp.dot(gated_out, out_weight, preferred_element_type=jn...  28.7 us
    all_gather x1, waiting for transfers between devices, on_device(): piece_rows = lax.all_gather(mixer_in, 'head', axis=0, tiled=True)  27.1 us
  transfers between devices with their start and end apart: 6, of which 5 were waited for; matrix products, arithmetic and copies ran while one was open for 3% of the time, Pallas kernels for 0%

commit v1 on v0

--- a/solution.py
+++ b/solution.py
@@ -7,6 +7,11 @@
 DK = 128
 epsilon = 1e-06
 exact_precision = lax.Precision.HIGHEST
+
+
+def tiled_gather(x, axis, dim):
+    copies = jnp.concatenate([x] * lax.axis_size(axis), axis=dim)
+    return lax.all_to_all(copies, axis, dim, dim, tiled=True)
 
 
 def passed_along(value, axis, steps):
@@ -191,7 +196,7 @@
         stream.astype(jnp.float32) + moe_out.astype(jnp.float32), mixer_gain
     ).astype(jnp.bfloat16)
     weight_list = (query_weight, key_weight, value_weight, output_gate, beta_weight, decay_weight)
-    piece_rows = lax.all_gather(mixer_in, "head", axis=0, tiled=True)
+    piece_rows = tiled_gather(mixer_in, "head", 0)
     projected = jnp.concatenate(
         [jnp.dot(piece_rows, matrix, preferred_element_type=jnp.float32) for matrix in weight_list],
         axis=1,

time: 859 us -> 864 us (level)
    all_gather x1 -> x0, waiting for transfers between devices: 27.1 us -> none  [on_device(): piece_rows = lax.all_gather(mixer_in, 'head', axis=0, tiled=True)]
    all_to_all x0 -> x1, waiting for transfers between devices: none -> 24.2 us  [tiled_gather(): return lax.all_to_all(copies, axis, dim, dim, tiled=True)]
where the time goes in v1:
time: 864 us; the launch traced here: 857 us
  waiting for transfers between devices  204 us (24%)
  matrix products  196 us (23%)
  other arithmetic  190 us (22%)
  local copies, waits for them, and re-layouts  151 us (17%)
  blocking collectives  87.2 us (10%)
  between operations  14.9 us (2%)
  starting transfers between devices  12.7 us (1%)
    another operation x2, other arithmetic, block_terms(): jax.scipy.linalg.solve_triangular(system, targets, lower=True, unit_diago...  159 us
    all_to_all x1, blocking collectives, on_device(): lax.all_to_all(outgoing, ('ctx', 'head'), split_axis=0, concat_axis=0, ti...  87.2 us
    all_gather x2, waiting for transfers between devices, prefix(): lax.all_gather(part.astype(kind), axis)  86.5 us
    all_to_all x1, waiting for transfers between devices, on_device(): lax.all_to_all(jnp.einsum('nesh,ehd->nesd', hidden, expert_down, preferre...  64.3 us
    dot_general x32, matrix products, compose(): jnp.einsum('hij,hjk->hik', later[0], earlier[1], precision=exact_precision)  40.5 us
    scatter x1, local copies, waits for them, and re-layouts, on_device(): outgoing = jnp.zeros((experts_all * capacity, model_width), jnp.bfloat16)...  34.2 us
    reduce_scatter x1, waiting for transfers between devices, on_device(): lax.psum_scatter(jnp.dot(gated_out, out_weight, preferred_element_type=jn...  28.7 us
    all_to_all x1, waiting for transfers between devices, tiled_gather(): return lax.all_to_all(copies, axis, dim, dim, tiled=True)  24.2 us
  transfers between devices with their start and end apart: 6, of which 5 were waited for; matrix products, arithmetic and copies ran while one was open for 3% of the time, Pallas kernels for 0%

profile of v1, /device:TPU:1, one launch (start us, length us, event | category | flops | bytes accessed | tf_op | source)
XLA Modules:
  0.0 857.2 jit_solution(3957865146737101263)
XLA Ops:
  11.0 1.8 add_add_fusion
  12.9 1.8 copy.130
  15.2 1.7 fusion.90
  17.1 34.2 %scatter_custom_fusion = bf16[1536,2048]{1,0:T(8,128)(2,1)} fusion(s32[1280]{0:T(1024)S(1)} %fusion.111, bf16[128,2048]{1,0:T(8,128)(2,1)S(1)} %fusion.102, s32[2048]{0:T(1024)S(1)} %pad_clamp_fusion.1, bf16[]{:T(256)} %constant.111.clone.1), kind=kCustom, calls=%fused_computation.65 | custom fusion | bytes 6291458 | tf_op jit(solution)/shard_map/scatter | solution.py:171
  51.3 11.0 %reshape.243 = bf16[128,2,6,2048]{3,2,1,0:T(8,128)(2,1)} reshape(bf16[1536,2048]{1,0:T(8,128)(2,1)} %scatter_custom_fusion) | data formatting | bytes 12582912 | tf_op jit(solution)/shard_map/reshape | solution.py:173
  62.3 9.6 %copy.131 = bf16[128,2,6,2048]{3,1,2,0:T(2,128)(2,1)S(1)} copy(bf16[128,2,6,2048]{3,2,1,0:T(8,128)(2,1)} %reshape.243) | data formatting | bytes 12582912 | tf_op jit(solution)/shard_map/reshape | solution.py:173
  72.0 87.2 %all_to_all.22 = bf16[128,2,6,2048]{3,1,2,0:T(2,128)(2,1)S(1)} all-to-all(bf16[128,2,6,2048]{3,1,2,0:T(2,128)(2,1)S(1)} %copy.131), channel_id=1, replica_groups=mesh['ctx'=32,'head'=4] {'ctx','head'}, dimensions={0} | all-to-all | bytes 12582912 | tf_op jit(solution)/shard_map/all_to_all | solution.py:174
  159.2 2.6 copy-done.6
  161.8 8.6 %fusion.48 = f32[2,128,6,512]{3,1,2,0:T(8,128)} fusion(bf16[128,2,6,2048]{3,1,2,0:T(2,128)(2,1)S(1)} %all_to_all.22, bf16[2,2048,512]{2,1,0:T(8,128)(2,1)S(1)} %copy-done.21), kind=kOutput, calls=%fused_computation.61 | convolution fusion | flops 3221225472 | bytes 13631488 | tf_op jit(solution)/shard_map/nesd,edh->nesh/dot_general | solution.py:178
  170.4 19.9 %convert_bitcast_fusion = bf16[128,2,6,2048]{3,0,2,1:T(8,128)(2,1)} fusion(bf16[2,512,2048]{2,1,0:T(8,128)(2,1)} %param.31, f32[2,128,6,512]{3,1,2,0:T(8,128)} %fusion.48, bf16[2,2048,512]{2,1,0:T(8,128)(2,1)} %param.29, bf16[128,2,6,2048]{3,1,2,0:T(2,128)(2,1)} %copy-done.6), kind=kOutput, calls=%fused_computation.60 | convolution fusion | flops 6450315264 | bytes 24117248 | tf_op jit(solution)/shard_map/nesh,ehd->nesd/dot_general | solution.py:181
  190.3 12.7 %copy.134 = bf16[128,2,6,2048]{3,1,2,0:T(2,128)(2,1)} copy(bf16[128,2,6,2048]{3,0,2,1:T(8,128)(2,1)} %convert_bitcast_fusion) | data formatting | bytes 12582912 | tf_op jit(solution)/shard_map/convert_element_type | solution.py:183
  203.0 5.3 all-to-all-start.1
  210.1 10.1 %gather_fusion.1 = f32[1280]{0:T(1024)S(1)} fusion(f32[128,256]{1,0:T(8,128)S(1)} %fusion.119, s32[1280]{0:T(1024)S(1)} %reshape.279), kind=kCustom, calls=%fused_computation.2 | custom fusion | bytes 20480 | tf_op jit(solution)/shard_map/jit(take_along_axis)/gather | solution.py:158
  220.6 64.3 %all-to-all-done.1 = bf16[128,2,6,2048]{3,1,2,0:T(2,128)(2,1)} async-done(((bf16[128,2,6,2048]{3,1,2,0:T(2,128)(2,1)}), bf16[128,2,6,2048]{3,1,2,0:T(2,128)(2,1)}, u32[]{:S(2)}, u32[]{:S(2)}) %all-to-all-start.1) | async-done | bytes 6291488 | tf_op jit(solution)/shard_map/all_to_all | solution.py:180
  285.0 10.4 %copy.135 = bf16[128,2,6,2048]{3,2,1,0:T(8,128)(2,1)} copy(bf16[128,2,6,2048]{3,1,2,0:T(2,128)(2,1)} %all-to-all-done.1) | data formatting | bytes 12582912 | tf_op jit(solution)/shard_map/all_to_all | solution.py:180
  295.4 11.0 %reshape.244 = bf16[1536,2048]{1,0:T(8,128)(2,1)} reshape(bf16[128,2,6,2048]{3,2,1,0:T(8,128)(2,1)} %copy.135) | data formatting | bytes 12582912 | tf_op jit(solution)/shard_map/reshape | solution.py:189
  306.4 14.4 %gather_fusion = bf16[1280,2048]{1,0:T(8,128)(2,1)} fusion(bf16[1536,2048]{1,0:T(8,128)(2,1)} %reshape.244, s32[2048]{0:T(1024)S(1)} %pad_clamp_fusion), kind=kCustom, calls=%fused_computation.1 | custom fusion | bytes 10490880 | tf_op jit(solution)/shard_map/gather | solution.py:189
  320.8 10.5 %reshape.260 = f32[128,10,2048]{2,1,0:T(8,128)} reshape(bf16[1280,2048]{1,0:T(8,128)(2,1)} %gather_fusion) | data formatting | bytes 15728640 | tf_op jit(solution)/shard_map/convert_element_type | solution.py:192
  331.3 9.6 %multiply_reduce_fusion = bf16[128,2048]{1,0:T(8,128)(2,1)S(1)} fusion(f32[128,10,2048]{2,1,0:T(8,128)} %reshape.260, f32[128,10]{1,0:T(8,128)S(1)} %copy.125), kind=kLoop, calls=%fused_computation.59 | loop fusion | flops 4980736 | bytes 11015168 | tf_op jit(solution)/shard_map/reduce_sum | solution.py:192
  341.5 1.6 pad_maximum_fusion.1
  343.1 4.6 all-to-all-start.2
  349.3 24.2 %all-to-all-done.2 = bf16[4,128,2048]{2,1,0:T(8,128)(2,1)} async-done(((bf16[4,128,2048]{2,1,0:T(8,128)(2,1)}), bf16[4,128,2048]{2,1,0:T(8,128)(2,1)}, u32[]{:S(2)}, u32[]{:S(2)}) %all-to-all-start.2) | async-done | bytes 2097184 | tf_op jit(solution)/shard_map/all_to_all | solution.py:14
  373.5 3.6 convolution_convert_fusion.2
  377.1 2.4 convolution_convert_fusion.3
  379.5 2.4 convolution_convert_fusion.4
  381.9 1.7 pad_maximum_fusion.2
  383.8 2.4 collective-permute-start
  386.2 2.3 fusion.110
  388.5 2.3 fusion.94
  393.0 6.5 divide_multiply_fusion
  405.0 3.5 fusion.88
  408.6 158.7 %custom-call.4 = f32[4,8,1,64,64]{3,4,2,1,0:T(8,128)} custom-call(f32[4,8,1,64,64]{4,3,2,1,0:T(8,128)} %fusion.88), custom_call_target="InvertDiagBlocksLowerTriangular" | custom-call | tf_op jit(solution)/shard_map/vmap(vmap(jit(_solve_triangular)))/triangular_solve | solution.py:67
  569.9 1.7 broadcast_multiply_fusion
  572.1 2.4 fusion.70
  574.5 1.6 slice_bitcast_fusion
  576.1 2.8 fusion.84
  578.9 100.5 %while.31 = (s32[]{:T(128)}, f32[4,128,128]{2,1,0:T(8,128)S(1)}, f32[4,128,128]{2,1,0:T(8,128)S(1)}, f32[8,4,64,128]{3,2,0,1:T(8,128)}, f32[8,4,64,128]{3,2,0,1:...) while((s32[]{:T(128)}, f32[4,128,128]{2,1,0:T(8,128)S(1)}, ...), condition=%wide.region_12.13_spmd.clone, body=%wide.region_11.12_spmd.clone.sunk | while | flops 352878592 | bytes 4855501 | solution.py:114
  581.4 1.9 fusion.192
  585.8 1.9 fusion.194
  594.0 1.9 fusion.192
  598.4 1.9 fusion.194
  602.5 1.5 convolution_subtract_fusion.6
  606.6 1.9 fusion.192
  610.9 1.9 fusion.194
  619.1 1.9 fusion.192
  623.5 1.9 fusion.194
  631.7 1.9 fusion.192
  636.0 1.9 fusion.194
  644.2 1.9 fusion.192
  648.6 1.9 fusion.194
  656.8 1.9 fusion.192
  661.2 1.9 fusion.194
  665.3 1.5 convolution_subtract_fusion.6
  669.4 1.9 fusion.192
  673.7 1.9 fusion.194
  677.9 1.5 convolution_subtract_fusion.6
  681.2 4.3 convolution_convert_fusion.1
  685.5 1.6 copy.149
  687.1 38.6 %all-gather.5.cloned.1.call-done = bf16[128,128,128]{2,1,0:T(8,128)(2,1)} async-done(((bf16[4,128,128]{2,1,0:T(8,128)(2,1)}), bf16[128,128,128]{2,1,0:T(8,128)(2,1)}) %all-gather.5.cloned.1.call-update) | async-done | bytes 4194320 | tf_op jit(solution)/shard_map/all_gather | solution.py:26
  725.6 48.0 %all-gather.7.cloned.1.call-done = bf16[128,128,128]{2,1,0:T(8,128)(2,1)} async-done(((bf16[4,128,128]{2,1,0:T(8,128)(2,1)}), bf16[128,128,128]{2,1,0:T(8,128)(2,1)}) %all-gather.7.cloned.1.call-update) | async-done | bytes 4194320 | tf_op jit(solution)/shard_map/all_gather | solution.py:26
  773.6 42.3 %while.32 = (s32[]{:T(128)}, f32[4,128,128]{2,1,0:T(8,128)S(1)}, s32[]{:T(128)}, bf16[32,4,128,128]{3,2,1,0:T(8,128)(2,1)}, bf16[32,4,128,128]{3,2,1,0:T(8,128)(2,1)}, /*index=5*/s32[]{:T(128)}, s32[]{:T(128)}) while((s32[]{:T(128)}, f32[4,128,128]{2,1,0:T(8,128)S(1)}, s32[]{:T(128)}, bf16[32,4,128,128]{3,2,1,0:T(8,128)(2,1)}, ...), condition=%wide.region_14.15_spmd.clone, body=%wide.region_13.14_spmd.clone.sunk | while | flops 100990976 | bytes 1575519 | solution.py:43
  815.9 2.4 multiply_reduce_fusion.1
  818.8 2.6 convolution_convert_fusion
  821.5 28.7 %reduce-scatter.2.cloned.1.call-done = bf16[128,2048]{1,0:T(8,128)(2,1)} async-done(((bf16[512,2048]{1,0:T(8,128)(2,1)}), bf16[128,2048]{1,0:T(8,128)(2,1)}) %reduce-scatter.2.cloned.1.call-update) | async-done | bytes 524304 | tf_op jit(solution)/shard_map/reduce_scatter | solution.py:264
  (240 shorter events, 127.7 us)
Async XLA Ops:
  7.2 811.6 %copy-start = (bf16[512,2048]{1,0:T(8,128)(2,1)S(1)}, bf16[512,2048]{1,0:T(8,128)(2,1)}, u32[]{:S(2)}) copy-start(bf16[512,2048]{1,0:T(8,128)(2,1)} %param.45) | copy-start | bytes 6291460
  9.6 1.3 copy-start.4
  12.8 2.1 copy-start.5
  12.8 4.1 copy-start.14
  71.9 89.9 %copy-start.21 = (bf16[2,2048,512]{2,1,0:T(8,128)(2,1)S(1)}, bf16[2,2048,512]{2,1,0:T(8,128)(2,1)}, u32[]{:S(2)}) copy-start(bf16[2,2048,512]{2,1,0:T(8,128)(2,1)} %param.30) | copy-start | bytes 12582916
  159.2 2.6 copy-start.6
  203.0 5.3 copy-start.11
  203.0 81.9 %all-to-all-start.1 = ((bf16[128,2,6,2048]{3,1,2,0:T(2,128)(2,1)}), bf16[128,2,6,2048]{3,1,2,0:T(2,128)(2,1)}, u32[]{:S(2)}, u32[]{:S(2)}) async-start(bf16[128,2,6,2048]{3,1,2,0:T(2,128)(2,1)} %copy.134), calls=%async_computation.1 | async-start | bytes 12582912 | tf_op jit(solution)/shard_map/all_to_all | solution.py:180
  331.3 9.9 %copy-start.15 = (f32[2048]{0:T(1024)S(1)}, f32[2048]{0:T(1024)}, u32[]{:S(2)}) copy-start(f32[2048]{0:T(1024)} %param.32) | copy-start | bytes 24580
  340.9 2.1 copy-start.7
  343.1 4.7 copy-start.17
  343.1 4.8 copy-start.18
  343.1 4.8 copy-start.16
  343.1 5.5 copy-start.24
  343.1 30.4 %all-to-all-start.2 = ((bf16[4,128,2048]{2,1,0:T(8,128)(2,1)}), bf16[4,128,2048]{2,1,0:T(8,128)(2,1)}, u32[]{:S(2)}, u32[]{:S(2)}) async-start(bf16[4,128,2048]{2,1,0:T(8,128)(2,1)} %bitcast.246), calls=%async_computation.2 | async-start | bytes 4194304 | tf_op jit(solution)/shard_map/all_to_all | solution.py:14
  347.7 377.9 %all-gather.5.cloned.1.call-start = ((), (), s32[]{:S(2)}) async-start(), calls=%async_computation.5 | async-start | bytes 4325376 | tf_op jit(solution)/shard_map/all_gather | solution.py:26
  373.5 3.6 copy-start.22
  377.1 2.5 copy-start.23
  381.9 4.3 copy-start.12
  381.9 4.2 copy-start.20
  383.6 4.9 copy-start.13
  383.8 9.2 %collective-permute-start = (bf16[3,1024]{0,1:T(8,128)(2,1)S(1)}, bf16[3,1024]{0,1:T(8,128)(2,1)S(1)}, u32[]{:S(2)}, u32[]{:S(2)}) collective-permute-start(bf16[3,1024]{0,1:T(8,128)(2,1)S(1)} %slice.81), channel_id=1, source_target_pairs={{0,4},{4,8},{8,12},{12,16},{16,20},{20,24},{24,28},{28,32},{32,36}... | collective-permute-start | bytes 18440 | tf_op jit(solution)/shard_map/ppermute | solution.py:20
  399.5 1.3 copy-start.1
  402.8 164.4 %slice-start = ((f32[512,1024]{0,1:T(8,128)}), f32[512,512]{0,1:T(8,128)S(1)}, s32[]{:S(2)}) async-start(f32[512,1024]{0,1:T(8,128)} %copy-done.1), calls=%async_computation.7 | async-start | bytes 2097152 | tf_op jit(solution)/shard_map/slice | solution.py:228
  404.0 1.0 copy-start.2
  568.5 1.4 copy-start.3
  569.9 1.7 copy-start.8
  569.9 2.2 copy-start.9
  680.1 93.5 %all-gather.7.cloned.1.call-start = ((), (), s32[]{:S(2)}) async-start(), calls=%async_computation.6 | async-start | bytes 4325376 | tf_op jit(solution)/shard_map/all_gather | solution.py:26
  680.9 169.3 %reduce-scatter.2.cloned.1.call-start = ((), (), s32[]{:S(2)}) async-start(), calls=%async_computation.4 | async-start | bytes 2621440 | tf_op jit(solution)/shard_map/reduce_scatter | solution.py:264
  815.9 2.4 copy-start.10
  815.9 2.4 copy-start.19
Sparse Core Ops, SparseCore 0:
  680.2 45.3 all-gather.4
  727.9 45.6 all-gather.6
  821.6 28.5 reduce-scatter.1
